TPU v7x, 256 devices: a whole 4x4x8 slice. The times are simulated.
256 devices in a mesh: row: 32 (over z_lo, x, core), col: 8 (over z_hi, y).
Axes of the slice: x: 4, y: 4, z: 8 (z_hi: 2, z_lo: 4; z = z_hi * 4 + z_lo), core: 2. Of those that a mesh axis runs over, the one named last changes fastest.
Arguments:
- activations: bfloat16 [1024, 16384], P('col', 'row'), may hold values from 0 to 2
- blocks_one: bfloat16 [32, 8, 64, 128, 128], P('row', 'col'), may hold values from -0.09375 to 0.09375
- pattern_one: int32 [32, 8, 64], P('row', 'col'), may hold values from 0 to 63, as said below
- count_one: int32 [32, 8], P('row', 'col'), may hold values from 1 to 64, as said below
- blocks_two: bfloat16 [8, 32, 64, 128, 128], P('col', 'row'), may hold values from -0.125 to 0.125
- pattern_two: int32 [8, 32, 64], P('col', 'row'), may hold values from 0 to 63, as said below
- count_two: int32 [8, 32], P('col', 'row'), may hold values from 1 to 64, as said below
Outputs:
- sparse_out: bfloat16 [1024, 16384], P('col', 'row')
Inputs may be any that keep to these rules, and one draw needn't show every extreme that they name: `pattern_one`: in each tile the slots below its count hold distinct positions; slots at or above the count hold positions in range whose blocks are not part of the weights. `count_one`: some tile has exactly 64 live slots. `pattern_two`: in each tile the slots below its count hold distinct positions; slots at or above the count hold positions in range whose blocks are not part of the weights. `count_two`: some tile has exactly 64 live slots.
All inputs are finite; a program needn't handle non-finite values.
Results may differ from a plain program's by a relative error of at most 0.0053.
Values may be sent and summed in bfloat16 or wider, within the bound.
A program may use at most 64 MiB of HBM per device.

v0:
```python
import jax
import jax.numpy as jnp
from jax import lax
from jax.sharding import Mesh
from jax.sharding import PartitionSpec as P

N = 16384
ROW = ("row_0", "row_1", "row_2")
bias_value = -0.3


def from_everyone(array, axis):
    copies = jnp.broadcast_to(array, (lax.axis_size(axis), *array.shape))
    return lax.all_to_all(copies, axis, split_axis=0, concat_axis=0, tiled=True)


def joined_along(pieces, dim):
    pieces = jnp.moveaxis(pieces, 0, dim)
    shape = pieces.shape
    return pieces.reshape(*shape[:dim], shape[dim] * shape[dim + 1], *shape[dim + 2 :])


def gather_directly(array, axis, dim):
    pieces = from_everyone(array, axis)
    return joined_along(pieces, dim)


def split_up(array, dim, devices):
    before, after = (array.shape[:dim], array.shape[dim + 1 :])
    return jnp.moveaxis(array.reshape(*before, devices, -1, *after), dim, 0)


def scatter_pairs(array, chips, core, dim):
    sizes = (lax.axis_size(chips), lax.axis_size(core))
    pieces = split_up(array, dim, sizes[0] * sizes[1])
    inside = pieces.shape[1:]
    pieces = pieces.reshape(*sizes, *inside).swapaxes(0, 1).reshape(-1, *inside)
    pieces = lax.psum_scatter(pieces, core, scatter_dimension=0, tiled=True)
    return lax.psum_scatter(pieces, chips, scatter_dimension=0, tiled=True)[0]


def sum_at_owner(array, axis, dim):
    devices = lax.axis_size(axis)
    pieces = lax.all_to_all(split_up(array, dim, devices), axis, 0, 0, tiled=True)
    return jnp.sum(pieces, axis=0)


def build_tile(where, live, blocks, block_rows, block_cols):
    slots = blocks.shape[0]
    size = blocks.shape[-1]
    places = jnp.arange(block_rows * block_cols, dtype=jnp.int32)
    used = jnp.arange(slots, dtype=jnp.int32) < live
    onehot = ((places[:, None] == where[None, :]) & used[None, :]).astype(jnp.bfloat16)
    flat = blocks.reshape(slots, size * size)
    tiles = jnp.dot(onehot, flat, preferred_element_type=jnp.float32).astype(jnp.bfloat16)
    tiles = tiles.reshape(block_rows, block_cols, size, size).transpose(0, 2, 1, 3)
    return tiles.reshape(block_rows * size, block_cols * size)


def apply_blocks(panel, where, live, blocks, width):
    size = blocks.shape[-1]
    block_rows = panel.shape[1] // size
    block_cols = width // size
    tile = build_tile(where, live, blocks, block_rows, block_cols)
    return jnp.dot(panel, tile, preferred_element_type=jnp.float32)


def shards(activations, blocks_one, pattern_one, count_one, blocks_two, pattern_two, count_two):
    where_one = pattern_one.reshape(-1)
    live_one = count_one.reshape(())
    stored_one = blocks_one.reshape(blocks_one.shape[2:])
    where_two = pattern_two.reshape(-1)
    live_two = count_two.reshape(())
    stored_two = blocks_two.reshape(blocks_two.shape[2:])
    width_one = N // lax.axis_size("col")
    width_two = N // lax.axis_size(ROW)
    partial_one = apply_blocks(
        gather_directly(activations, "col", 0), where_one, live_one, stored_one, width_one
    )
    share = scatter_pairs(partial_one, ("row_0", "row_1"), "row_2", 0)
    hidden_share = jnp.maximum(share + bias_value, 0.0).astype(jnp.bfloat16)
    partial_two = apply_blocks(
        lax.all_gather(hidden_share, ROW, axis=0, tiled=True),
        where_two,
        live_two,
        stored_two,
        width_two,
    )
    result = sum_at_owner(partial_two, "col", 0)
    return jnp.maximum(result + bias_value, 0.0).astype(jnp.bfloat16)


def solution(mesh):
    split = Mesh(
        mesh.devices.reshape(4, 4, 2, mesh.shape["col"]), ("row_0", "row_1", "row_2", "col")
    )
    return jax.shard_map(
        shards,
        mesh=split,
        in_specs=(
            P("col", ROW),
            P(ROW, "col", None, None, None),
            P(ROW, "col", None),
            P(ROW, "col"),
            P("col", ROW, None, None, None),
            P("col", ROW, None),
            P("col", ROW),
        ),
        out_specs=P("col", ROW),
        check_vma=False,
    )
```

profile of v0, /device:TPU:32, one launch (start us, length us, event | category | flops | bytes accessed | tf_op | source)
XLA Modules:
  0.0 306.1 jit_solution(11263311072547643464)
XLA Ops:
  6.5 0.0 copy-start.2
  6.5 0.0 copy-start
  6.5 2.1 broadcast_in_dim.2
  8.7 10.2 %all-to-all-start = ((bf16[8,128,512]{2,1,0:T(8,128)(2,1)}), bf16[8,128,512]{2,1,0:T(8,128)(2,1)S(1)}, u32[]{:S(2)}, u32[]{:S(2)}) async-start(bf16[8,128,512]{2,1,0:T(8,128)(2,1)} %broadcast_in_dim.2), calls=%async_computation | async-start | bytes 2097152 | tf_op jit(solution)/shard_map/all_to_all | solution.py:14
  18.9 0.0 reduce-scatter.3.cloned.1.call-start
  19.6 0.0 copy-done.2
  19.6 0.0 copy-done
  19.6 1.7 fusion.7
  21.3 0.6 copy.13
  21.9 1.4 copy.9
  23.2 24.7 %all-to-all-done = bf16[8,128,512]{2,1,0:T(8,128)(2,1)S(1)} async-done(((bf16[8,128,512]{2,1,0:T(8,128)(2,1)}), bf16[8,128,512]{2,1,0:T(8,128)(2,1)S(1)}, u32[]{:S(2)}, u32[]{:S(2)}) %all-to-all-start) | async-done | bytes 1048608 | tf_op jit(solution)/shard_map/all_to_all | solution.py:14
  47.9 2.3 fusion.2
  50.3 3.8 %copy.10 = f32[16,2,32,2048]{3,2,0,1:T(8,128)} copy(f32[16,2,32,2048]{3,2,1,0:T(8,128)S(1)} %bitcast.48) | data formatting | bytes 16777216 | tf_op jit(solution)/shard_map/reshape;reshape | solution.py:37
  54.1 0.0 reduce-scatter.3.cloned.1.call-update
  54.1 0.0 reduce-scatter.5.cloned.1.call-start
  54.2 19.5 %reduce-scatter.3.cloned.1.call-done = f32[16,32,2048]{2,1,0:T(8,128)} async-done(((f32[32,32,2048]{2,1,0:T(8,128)}), f32[16,32,2048]{2,1,0:T(8,128)}) %reduce-scatter.3.cloned.1.call-update) | async-done | bytes 4194320 | tf_op jit(solution)/shard_map/reduce_scatter | solution.py:38
  73.7 0.0 copy-start.1
  73.7 0.0 copy-start.3
  73.7 0.0 reduce-scatter.5.cloned.1.call-update
  73.7 0.0 all-gather.3.cloned.1.call-start
  73.8 90.5 %reduce-scatter.5.cloned.1.call-done = f32[1,32,2048]{2,1,0:T(8,128)} async-done(((f32[16,32,2048]{2,1,0:T(8,128)}), f32[1,32,2048]{2,1,0:T(8,128)}) %reduce-scatter.5.cloned.1.call-update) | async-done | bytes 262160 | tf_op jit(solution)/shard_map/reduce_scatter | solution.py:39
  164.3 1.6 maximum_convert_fusion.1
  165.9 0.0 all-gather.3.cloned.1.call-update
  166.6 0.0 copy-done.1
  166.6 0.0 copy-done.3
  166.6 1.7 fusion.10
  168.3 0.6 copy.16
  168.9 1.8 copy.11
  170.7 2.2 reshape.51
  172.9 59.4 %all-gather.3.cloned.1.call-done = bf16[1,1024,2048]{2,1,0:T(8,128)(2,1)} async-done(((bf16[1,32,2048]{2,1,0:T(8,128)(2,1)}), bf16[1,1024,2048]{2,1,0:T(8,128)(2,1)}) %all-gather.3.cloned.1.call-update) | async-done | bytes 4194320 | tf_op jit(solution)/shard_map/all_gather | solution.py:83
  232.3 5.2 %fusion.21 = f32[8,128,512]{2,1,0:T(8,128)S(1)} fusion(bf16[8,128,2048]{2,1,0:T(8,128)(2,1)} %bitcast.57, bf16[2048,512,1]{1,0,2:T(8,128)(2,1)} %reshape.51), kind=kOutput, calls=%fused_computation.23 | convolution fusion | flops 2147483648 | bytes 8388608 | tf_op jit(solution)/shard_map/dot_general | solution.py:65
  237.5 61.1 %all_to_all.10 = f32[8,128,512]{2,1,0:T(8,128)S(1)} all-to-all(f32[8,128,512]{2,1,0:T(8,128)S(1)} %fusion.21), channel_id=1, replica_groups=mesh['row_0'=4,'row_1'=4,'row_2'=2,'col'=8] {'col'}, dimensions={0} | all-to-all | bytes 4194304 | tf_op jit(solution)/shard_map/all_to_all | solution.py:44
  298.7 0.2 reduce_sum.9
  298.9 0.7 maximum_convert_fusion
  (2 shorter events, 0.0 us)
Async XLA Ops:
  6.5 13.0 %copy-start.2 = (s32[1,1,64]{2,1,0:T(1,128)S(1)}, s32[1,1,64]{2,1,0:T(1,128)}, u32[]{:S(2)}) copy-start(s32[1,1,64]{2,1,0:T(1,128)} %param.9) | copy-start | bytes 772
  6.5 13.0 %copy-start = (bf16[1,1,64,128,128]{4,3,2,1,0:T(8,128)(2,1)S(1)}, bf16[1,1,64,128,128]{4,3,2,1,0:T(8,128)(2,1)}, u32[]{:S(2)}) copy-start(bf16[1,1,64,128,128]{4,3,2,1,0:T(8,128)(2,1)} %param.8) | copy-start | bytes 6291460
  8.7 39.3 %all-to-all-start = ((bf16[8,128,512]{2,1,0:T(8,128)(2,1)}), bf16[8,128,512]{2,1,0:T(8,128)(2,1)S(1)}, u32[]{:S(2)}, u32[]{:S(2)}) async-start(bf16[8,128,512]{2,1,0:T(8,128)(2,1)} %broadcast_in_dim.2), calls=%async_computation | async-start | bytes 2097152 | tf_op jit(solution)/shard_map/all_to_all | solution.py:14
  18.9 54.8 %reduce-scatter.3.cloned.1.call-start = ((), (), s32[]{:S(2)}) async-start(), calls=%async_computation.4 | async-start | bytes 12582912 | tf_op jit(solution)/shard_map/reduce_scatter | solution.py:38
  54.1 110.1 %reduce-scatter.5.cloned.1.call-start = ((), (), s32[]{:S(2)}) async-start(), calls=%async_computation.5 | async-start | bytes 4456448 | tf_op jit(solution)/shard_map/reduce_scatter | solution.py:39
  73.7 92.9 %copy-start.1 = (bf16[1,1,64,128,128]{4,3,2,1,0:T(8,128)(2,1)S(1)}, bf16[1,1,64,128,128]{4,3,2,1,0:T(8,128)(2,1)}, u32[]{:S(2)}) copy-start(bf16[1,1,64,128,128]{4,3,2,1,0:T(8,128)(2,1)} %param.11) | copy-start | bytes 6291460
  73.7 92.9 %copy-start.3 = (s32[1,1,64]{2,1,0:T(1,128)S(1)}, s32[1,1,64]{2,1,0:T(1,128)}, u32[]{:S(2)}) copy-start(s32[1,1,64]{2,1,0:T(1,128)} %param.12) | copy-start | bytes 772
  73.7 158.6 %all-gather.3.cloned.1.call-start = ((), (), s32[]{:S(2)}) async-start(), calls=%async_computation.6 | async-start | bytes 4325376 | tf_op jit(solution)/shard_map/all_gather | solution.py:83
Sparse Core Ops, SparseCore 0:
  54.2 19.4 reduce-scatter.2
  76.4 87.8 reduce-scatter.4
  166.3 65.9 all-gather.2
where the time goes:
time: 306 us
  waiting for transfers between devices  194 us (63%)
  blocking collectives  61.1 us (20%)
  between operations  14.5 us (5%)
  local copies, waits for them, and re-layouts  12.4 us (4%)
  matrix products  10.9 us (4%)
  starting transfers between devices  10.3 us (3%)
    reduce_scatter x1, waiting for transfers between devices, scatter_pairs(): return lax.psum_scatter(pieces, chips, scatter_dimension=0, tiled=True)[0]  90.5 us
    all_to_all x1, blocking collectives, sum_at_owner(): lax.all_to_all(split_up(array, dim, devices), axis, 0, 0, tiled=True)  61.1 us
    all_gather x1, waiting for transfers between devices, shards(): lax.all_gather(hidden_share, ROW, axis=0, tiled=True)  59.4 us
    all_to_all x1, waiting for transfers between devices, from_everyone(): return lax.all_to_all(copies, axis, split_axis=0, concat_axis=0, tiled=True)  24.7 us
    reduce_scatter x1, waiting for transfers between devices, scatter_pairs(): pieces = lax.psum_scatter(pieces, core, scatter_dimension=0, tiled=True)  19.5 us
    all_to_all x1, starting transfers between devices, from_everyone(): return lax.all_to_all(copies, axis, split_axis=0, concat_axis=0, tiled=True)  10.2 us
    dot_general x2, matrix products, apply_blocks(): return jnp.dot(panel, tile, preferred_element_type=jnp.float32)  7.53 us
  transfers between devices with their start and end apart: 4, of which 4 were waited for; matrix products, arithmetic and copies ran while one was open for 3% of the time, Pallas kernels for 0%

commit v1 on v0

--- a/solution.py
+++ b/solution.py
@@ -80,7 +80,9 @@
     share = scatter_pairs(partial_one, ("row_0", "row_1"), "row_2", 0)
     hidden_share = jnp.maximum(share + bias_value, 0.0).astype(jnp.bfloat16)
     partial_two = apply_blocks(
-        lax.all_gather(hidden_share, ROW, axis=0, tiled=True),
+        jnp.concatenate(
+            lax.all_to_all(jnp.stack([hidden_share] * lax.axis_size(ROW)), ROW, 0, 0), axis=0
+        ),
         where_two,
         live_two,
         stored_two,

time: 306 us -> 346 us (1.13)
  waiting for transfers between devices: 194 us -> 220 us
  starting transfers between devices: 10.3 us -> 22.6 us
    all_to_all x0 -> x1, waiting for transfers between devices: none -> 84.3 us  [shards(): lax.all_to_all(jnp.stack([hidden_share] * lax.axis_size(ROW)), ROW, 0, 0)]
    all_gather x1 -> x0, waiting for transfers between devices: 59.4 us -> none  [shards(): lax.all_gather(hidden_share, ROW, axis=0, tiled=True)]
    all_to_all x0 -> x1, starting transfers between devices: none -> 12.4 us  [shards(): lax.all_to_all(jnp.stack([hidden_share] * lax.axis_size(ROW)), ROW, 0, 0)]
where the time goes in v1:
time: 346 us; the launch traced here: 345 us
  waiting for transfers between devices  220 us (64%)
  blocking collectives  60.6 us (18%)
  starting transfers between devices  22.6 us (7%)
  local copies, waits for them, and re-layouts  15 us (4%)
  between operations  14.8 us (4%)
  matrix products  10.9 us (3%)
    reduce_scatter x1, waiting for transfers between devices, scatter_pairs(): return lax.psum_scatter(pieces, chips, scatter_dimension=0, tiled=True)[0]  90.9 us
    all_to_all x1, waiting for transfers between devices, shards(): lax.all_to_all(jnp.stack([hidden_share] * lax.axis_size(ROW)), ROW, 0, 0)  84.3 us
    all_to_all x1, blocking collectives, sum_at_owner(): lax.all_to_all(split_up(array, dim, devices), axis, 0, 0, tiled=True)  60.6 us
    all_to_all x1, waiting for transfers between devices, from_everyone(): return lax.all_to_all(copies, axis, split_axis=0, concat_axis=0, tiled=True)  24.7 us
    reduce_scatter x1, waiting for transfers between devices, scatter_pairs(): pieces = lax.psum_scatter(pieces, core, scatter_dimension=0, tiled=True)  19.5 us
    all_to_all x1, starting transfers between devices, shards(): lax.all_to_all(jnp.stack([hidden_share] * lax.axis_size(ROW)), ROW, 0, 0)  12.4 us
    all_to_all x1, starting transfers between devices, from_everyone(): return lax.all_to_all(copies, axis, split_axis=0, concat_axis=0, tiled=True)  10.2 us
    dot_general x2, matrix products, apply_blocks(): return jnp.dot(panel, tile, preferred_element_type=jnp.float32)  7.53 us
  transfers between devices with their start and end apart: 4, of which 4 were waited for; matrix products, arithmetic and copies ran while one was open for 3% of the time, Pallas kernels for 0%

profile of v1, /device:TPU:32, one launch (start us, length us, event | category | flops | bytes accessed | tf_op | source)
XLA Modules:
  0.0 345.3 jit_solution(8656115852275788094)
XLA Ops:
  6.5 0.0 copy-start.2
  6.5 0.0 copy-start
  6.5 2.1 broadcast_in_dim.2
  8.7 10.2 %all-to-all-start = ((bf16[8,128,512]{2,1,0:T(8,128)(2,1)}), bf16[8,128,512]{2,1,0:T(8,128)(2,1)S(1)}, u32[]{:S(2)}, u32[]{:S(2)}) async-start(bf16[8,128,512]{2,1,0:T(8,128)(2,1)} %broadcast_in_dim.2), calls=%async_computation | async-start | bytes 2097152 | tf_op jit(solution)/shard_map/all_to_all | solution.py:14
  18.9 0.0 reduce-scatter.3.cloned.1.call-start
  19.6 0.0 copy-done.2
  19.6 0.0 copy-done
  19.6 1.7 fusion.7
  21.3 0.6 copy.13
  21.9 1.4 copy.9
  23.2 24.7 %all-to-all-done = bf16[8,128,512]{2,1,0:T(8,128)(2,1)S(1)} async-done(((bf16[8,128,512]{2,1,0:T(8,128)(2,1)}), bf16[8,128,512]{2,1,0:T(8,128)(2,1)S(1)}, u32[]{:S(2)}, u32[]{:S(2)}) %all-to-all-start) | async-done | bytes 1048608 | tf_op jit(solution)/shard_map/all_to_all | solution.py:14
  47.9 2.3 fusion.2
  50.3 3.8 %copy.10 = f32[16,2,32,2048]{3,2,0,1:T(8,128)} copy(f32[16,2,32,2048]{3,2,1,0:T(8,128)S(1)} %bitcast.50) | data formatting | bytes 16777216 | tf_op jit(solution)/shard_map/reshape;reshape | solution.py:37
  54.1 0.0 reduce-scatter.3.cloned.1.call-update
  54.1 0.0 reduce-scatter.5.cloned.1.call-start
  54.2 19.5 %reduce-scatter.3.cloned.1.call-done = f32[16,32,2048]{2,1,0:T(8,128)} async-done(((f32[32,32,2048]{2,1,0:T(8,128)}), f32[16,32,2048]{2,1,0:T(8,128)}) %reduce-scatter.3.cloned.1.call-update) | async-done | bytes 4194320 | tf_op jit(solution)/shard_map/reduce_scatter | solution.py:38
  73.7 0.0 reduce-scatter.5.cloned.1.call-update
  73.7 90.9 %reduce-scatter.5.cloned.1.call-done = f32[1,32,2048]{2,1,0:T(8,128)} async-done(((f32[16,32,2048]{2,1,0:T(8,128)}), f32[1,32,2048]{2,1,0:T(8,128)}) %reduce-scatter.5.cloned.1.call-update) | async-done | bytes 262160 | tf_op jit(solution)/shard_map/reduce_scatter | solution.py:39
  164.7 1.0 fusion.13
  165.6 2.5 stack.5
  168.2 0.0 copy-start.1
  168.2 0.0 copy-start.3
  168.2 12.4 %all-to-all-start.1 = ((bf16[32,32,2048]{2,1,0:T(8,128)(2,1)}), bf16[32,32,2048]{2,1,0:T(8,128)(2,1)}, u32[]{:S(2)}, u32[]{:S(2)}) async-start(bf16[32,32,2048]{2,1,0:T(8,128)(2,1)} %stack.5), calls=%async_computation.3 | async-start | bytes 8388608 | tf_op jit(solution)/shard_map/all_to_all | solution.py:84
  181.2 0.0 copy-done.1
  181.2 0.0 copy-done.3
  181.2 1.7 fusion.10
  182.9 0.6 copy.16
  183.5 1.8 copy.11
  185.3 2.2 reshape.47
  187.5 84.3 %all-to-all-done.1 = bf16[32,32,2048]{2,1,0:T(8,128)(2,1)} async-done(((bf16[32,32,2048]{2,1,0:T(8,128)(2,1)}), bf16[32,32,2048]{2,1,0:T(8,128)(2,1)}, u32[]{:S(2)}, u32[]{:S(2)}) %all-to-all-start.1) | async-done | bytes 4194336 | tf_op jit(solution)/shard_map/all_to_all | solution.py:84
  271.8 5.2 %fusion.22 = f32[8,128,512]{2,1,0:T(8,128)S(1)} fusion(bf16[8,128,2048]{2,1,0:T(8,128)(2,1)} %bitcast.9, bf16[2048,512,1]{1,0,2:T(8,128)(2,1)} %reshape.47), kind=kOutput, calls=%fused_computation.24 | convolution fusion | flops 2147483648 | bytes 8388608 | tf_op jit(solution)/shard_map/dot_general | solution.py:65
  277.0 60.6 %all_to_all.15 = f32[8,128,512]{2,1,0:T(8,128)S(1)} all-to-all(f32[8,128,512]{2,1,0:T(8,128)S(1)} %fusion.22), channel_id=1, replica_groups=mesh['row_0'=4,'row_1'=4,'row_2'=2,'col'=8] {'col'}, dimensions={0} | all-to-all | bytes 4194304 | tf_op jit(solution)/shard_map/all_to_all | solution.py:44
  337.6 0.2 reduce_sum.9
  337.8 0.7 maximum_convert_fusion
  (2 shorter events, 0.0 us)
Async XLA Ops:
  6.5 13.0 %copy-start.2 = (s32[1,1,64]{2,1,0:T(1,128)S(1)}, s32[1,1,64]{2,1,0:T(1,128)}, u32[]{:S(2)}) copy-start(s32[1,1,64]{2,1,0:T(1,128)} %param.9) | copy-start | bytes 772
  6.5 13.0 %copy-start = (bf16[1,1,64,128,128]{4,3,2,1,0:T(8,128)(2,1)S(1)}, bf16[1,1,64,128,128]{4,3,2,1,0:T(8,128)(2,1)}, u32[]{:S(2)}) copy-start(bf16[1,1,64,128,128]{4,3,2,1,0:T(8,128)(2,1)} %param.8) | copy-start | bytes 6291460
  8.7 39.3 %all-to-all-start = ((bf16[8,128,512]{2,1,0:T(8,128)(2,1)}), bf16[8,128,512]{2,1,0:T(8,128)(2,1)S(1)}, u32[]{:S(2)}, u32[]{:S(2)}) async-start(bf16[8,128,512]{2,1,0:T(8,128)(2,1)} %broadcast_in_dim.2), calls=%async_computation | async-start | bytes 2097152 | tf_op jit(solution)/shard_map/all_to_all | solution.py:14
  18.9 54.8 %reduce-scatter.3.cloned.1.call-start = ((), (), s32[]{:S(2)}) async-start(), calls=%async_computation.5 | async-start | bytes 12582912 | tf_op jit(solution)/shard_map/reduce_scatter | solution.py:38
  54.1 110.5 %reduce-scatter.5.cloned.1.call-start = ((), (), s32[]{:S(2)}) async-start(), calls=%async_computation.6 | async-start | bytes 4456448 | tf_op jit(solution)/shard_map/reduce_scatter | solution.py:39
  168.2 13.0 %copy-start.1 = (bf16[1,1,64,128,128]{4,3,2,1,0:T(8,128)(2,1)S(1)}, bf16[1,1,64,128,128]{4,3,2,1,0:T(8,128)(2,1)}, u32[]{:S(2)}) copy-start(bf16[1,1,64,128,128]{4,3,2,1,0:T(8,128)(2,1)} %param.11) | copy-start | bytes 6291460
  168.2 13.1 %copy-start.3 = (s32[1,1,64]{2,1,0:T(1,128)S(1)}, s32[1,1,64]{2,1,0:T(1,128)}, u32[]{:S(2)}) copy-start(s32[1,1,64]{2,1,0:T(1,128)} %param.12) | copy-start | bytes 772
  168.2 103.7 %all-to-all-start.1 = ((bf16[32,32,2048]{2,1,0:T(8,128)(2,1)}), bf16[32,32,2048]{2,1,0:T(8,128)(2,1)}, u32[]{:S(2)}, u32[]{:S(2)}) async-start(bf16[32,32,2048]{2,1,0:T(8,128)(2,1)} %stack.5), calls=%async_computation.3 | async-start | bytes 8388608 | tf_op jit(solution)/shard_map/all_to_all | solution.py:84
Sparse Core Ops, SparseCore 0:
  54.2 19.4 reduce-scatter.2
  76.4 88.2 reduce-scatter.4
